TPU v7x, 32 devices: a whole 2x2x4 slice. The times are simulated.
32 devices in a mesh: groups: 2 (over y), edge: 4 (over z), expert: 2 (over x), sys: 2 (over core).
Axes of the slice: x: 2, y: 2, z: 4, core: 2. Of those that a mesh axis runs over, the one named last changes fastest.
Arguments:
- edge_inputs: bfloat16 [8, 1792, 1280], P(('groups', 'expert', 'sys'), 'edge'), parts along dimension 0, may hold values from -6 to 6
- out_grad: bfloat16 [8, 1792, 1152], P(('groups', 'expert', 'sys'), 'edge'), parts along dimension 0, may hold values from -6 to 6
- expert_weights: bfloat16 [32, 1280, 1152], P('expert', 'edge'), may hold values from -0.15625 to 0.15625
- coef_table: float32 [16, 32], replicated, may hold values from 0.05 to 0.5
- system_kind: int32 [8], P('groups'), parts along dimension 0, may hold values from 0 to 15
- edge_counts: int32 [8], P('groups'), parts along dimension 0, may hold values from 896 to 1792, as said below
Outputs:
- input_grad: bfloat16 [8, 1792, 1280], P(('groups', 'expert', 'sys'), 'edge'), parts along dimension 0
- weight_grad: bfloat16 [64, 1280, 1152], P(('groups', 'expert'), 'edge'), parts along dimension 0
There are 2 independent parts, one for each index of `groups`. A program takes and returns all parts, laid end to end along the dimension named above; an argument that names none is the same for every part. Nothing has to cross between parts.
Inputs may be any that keep to these rules, and one draw needn't show every extreme that they name: `edge_counts`: the live edges of a system are its first ones. One system has all 1792 slots live and another exactly half of them.
All inputs are finite; a program needn't handle non-finite values.
Results may differ from a plain program's by a relative error of at most 0.018.
Values may be sent and summed in bfloat16 or wider, within the bound.
No kernel may reach another device: no remote copies, remote signals or barrier semaphores. Data moves between devices by JAX's collectives and lax.ppermute only.
A program may use at most 128 MiB of HBM per device.

v0:
```python
import math
import jax
import jax.numpy as jnp
from jax import lax
from jax.sharding import PartitionSpec as P


def body(edge_inputs, out_grad, expert_weights, coef_table, system_kind, edge_counts):
    highest = lax.Precision.HIGHEST
    edge_size = lax.axis_size("edge")
    expert_size = lax.axis_size("expert")
    sys_size = lax.axis_size("sys")
    edge_at = lax.axis_index("edge")
    expert_at = lax.axis_index("expert")
    sys_at = lax.axis_index("sys")
    systems = system_kind.shape[0]
    kinds = coef_table.shape[0]
    exp_local = expert_weights.shape[0]
    row_count = expert_weights.shape[1]
    width_out = expert_weights.shape[2]
    edge_rows = out_grad.shape[1]
    onehot = (system_kind[:, None] == jnp.arange(kinds, dtype=jnp.int32)[None, :]).astype(
        jnp.float32
    )
    coeffs = jnp.dot(onehot, coef_table, precision=highest)
    own_system = expert_at * sys_size + sys_at
    picked = jnp.arange(systems, dtype=jnp.int32) == own_system
    own_count = jnp.sum(jnp.where(picked, edge_counts, 0))
    positions = edge_at * edge_rows + jnp.arange(edge_rows, dtype=jnp.int32)
    masked_grad = jnp.where(
        (positions < own_count)[:, None], out_grad[0], jnp.zeros((), jnp.bfloat16)
    )
    features = edge_inputs[0]
    by_block = coeffs.reshape(expert_size, sys_size, -1)
    same_sys = lax.dynamic_slice_in_dim(by_block, sys_at, 1, 1)[:, 0, :]
    own_coeffs = lax.dynamic_slice_in_dim(same_sys, expert_at * exp_local, exp_local, 1)
    partials = jnp.sum(
        own_coeffs[:, :, None, None] * expert_weights.astype(jnp.float32)[None], axis=1
    ).astype(jnp.bfloat16)
    merged_rows = jnp.sum(
        lax.all_to_all(partials, "expert", split_axis=0, concat_axis=0, tiled=True).astype(
            jnp.float32
        ),
        axis=0,
    ).astype(jnp.bfloat16)
    product = lax.dot_general(
        masked_grad,
        lax.all_gather(merged_rows, "edge", axis=0, tiled=True),
        (((1,), (1,)), ((), ())),
        preferred_element_type=jnp.float32,
    )
    input_grad = product.astype(jnp.bfloat16)
    system_rows = lax.psum_scatter(
        lax.dot_general(
            features, masked_grad, (((0,), (0,)), ((), ())), preferred_element_type=jnp.float32
        ).astype(jnp.bfloat16),
        "edge",
        scatter_dimension=0,
        tiled=True,
    )
    local_coeffs = lax.dynamic_slice_in_dim(coeffs, expert_at * exp_local, exp_local, 1).T
    block_rows = lax.all_gather(system_rows[None], ("expert", "sys"), axis=0, tiled=True)
    span_rows = block_rows.shape[0]
    flat_rows = block_rows.reshape(span_rows, -1).astype(jnp.float32)
    folded = jnp.dot(local_coeffs, flat_rows, precision=highest)
    scale_factor = 1.0 / math.sqrt(edge_rows * edge_size)
    weight_grad = (
        (folded * scale_factor).reshape(exp_local, row_count, width_out).astype(jnp.bfloat16)
    )
    return (input_grad[None], weight_grad)


def solution(mesh):
    return jax.shard_map(
        body,
        mesh=mesh,
        in_specs=(
            P(("groups", "expert", "sys"), "edge", None),
            P(("groups", "expert", "sys"), "edge", None),
            P("expert", "edge", None),
            P(),
            P("groups"),
            P("groups"),
        ),
        out_specs=(
            P(("groups", "expert", "sys"), "edge", None),
            P(("groups", "expert"), "edge", None),
        ),
        check_vma=False,
    )
```

profile of v0, /device:TPU:0, one launch (start us, length us, event | category | flops | bytes accessed | tf_op | source)
XLA Modules:
  0.0 198.3 jit_solution(15670721173112743282)
XLA Ops:
  7.2 0.0 copy-start
  7.2 0.0 reduce-scatter.4.cloned.1.call-start
  7.2 1.4 fusion.13
  8.6 0.7 add_compare_fusion
  9.3 0.0 copy-done
  9.3 4.7 %fusion.1 = bf16[1280,1152]{0,1:T(8,128)(2,1)} fusion(bf16[1,448,1280]{2,1,0:T(8,128)(2,1)S(1)} %copy-done, bf16[1,448,1152]{2,1,0:T(8,128)(2,1)} %param.7, pred[448]{0:T(512)(128)(4,1)S(1)} %add_compare_fusion), kind=kOutput, calls=%fused_computation.4 | convolution fusion | flops 1323196416 | bytes 5128640 | tf_op jit(solution)/shard_map/dot_general | solution.py:54
  13.9 5.4 %copy.11 = bf16[1280,1152]{1,0:T(8,128)(2,1)} copy(bf16[1280,1152]{0,1:T(8,128)(2,1)} %fusion.1) | data formatting | bytes 5898240
  19.4 0.0 reduce-scatter.4.cloned.1.call-update
  19.4 0.0 all-gather.4.cloned.1.call-start
  19.5 0.0 copy-start.3
  19.5 0.0 copy-start.4
  19.5 13.6 %convert_element_type.25 = f32[16,320,1152]{2,1,0:T(8,128)} convert(bf16[16,320,1152]{2,1,0:T(8,128)(2,1)} %param.8) | non-fusion elementwise | flops 5898240 | bytes 35389440 | tf_op jit(solution)/shard_map/convert_element_type | solution.py:38
  33.1 0.0 copy-done.3
  33.1 0.0 copy-done.4
  33.1 0.2 fusion.11
  33.3 0.1 constant_dynamic-slice_fusion
  33.4 13.5 %multiply_reduce_fusion = bf16[2,320,1152]{2,1,0:T(8,128)(2,1)S(1)} fusion(f32[16,320,1152]{2,1,0:T(8,128)} %convert_element_type.25, f32[2,16]{1,0:T(2,128)S(1)} %bitcast.24), kind=kLoop, calls=%fused_computation.2 | loop fusion | flops 22855680 | bytes 25067648 | tf_op jit(solution)/shard_map/reduce_sum | solution.py:37
  46.8 0.0 copy-start.2
  46.9 22.3 %all_to_all.5 = bf16[2,320,1152]{2,1,0:T(8,128)(2,1)S(1)} all-to-all(bf16[2,320,1152]{2,1,0:T(8,128)(2,1)S(1)} %multiply_reduce_fusion), channel_id=1, replica_groups=mesh['groups'=2,'edge'=4,'expert'=2,'sys'=2] {'expert'}, dimensions={0} | all-to-all | bytes 2949120 | tf_op jit(solution)/shard_map/all_to_all | solution.py:41
  69.2 1.3 reduce_sum.32
  70.5 0.0 all-gather.4.cloned.1.call-update
  70.5 0.0 all-gather.6.cloned.1.call-start
  70.6 9.0 %reduce-scatter.4.cloned.1.call-done = bf16[320,1152]{1,0:T(8,128)(2,1)} async-done(((bf16[1280,1152]{1,0:T(8,128)(2,1)}), bf16[320,1152]{1,0:T(8,128)(2,1)}) %reduce-scatter.4.cloned.1.call-update) | async-done | bytes 737296 | tf_op jit(solution)/shard_map/reduce_scatter | solution.py:53
  79.6 0.0 all-gather.6.cloned.1.call-update
  79.7 62.1 %all-gather.4.cloned.1.call-done = bf16[1280,1152]{1,0:T(8,128)(2,1)} async-done(((bf16[320,1152]{1,0:T(8,128)(2,1)}), bf16[1280,1152]{1,0:T(8,128)(2,1)}) %all-gather.4.cloned.1.call-update) | async-done | bytes 2949136 | tf_op jit(solution)/shard_map/all_gather | solution.py:48
  141.8 0.0 copy-done.2
  141.8 4.6 %fusion.2 = bf16[1,448,1280]{2,1,0:T(8,128)(2,1)} fusion(bf16[1280,1152]{1,0:T(8,128)(2,1)} %all-gather.4.cloned.1.call-done, bf16[1,448,1152]{2,1,0:T(8,128)(2,1)S(1)} %copy-done.2, pred[448]{0:T(512)(128)(4,1)S(1)} %add_compare_fusion), kind=kOutput, calls=%fused_computation.6 | convolution fusion | flops 1322295296 | bytes 5128640 | tf_op jit(solution)/shard_map/dot_general | solution.py:46
  146.3 23.1 %all-gather.6.cloned.1.call-done = bf16[1280,1152]{1,0:T(8,128)(2,1)} async-done(((bf16[320,1152]{1,0:T(8,128)(2,1)}), bf16[1280,1152]{1,0:T(8,128)(2,1)}) %all-gather.6.cloned.1.call-update) | async-done | bytes 2949136 | tf_op jit(solution)/shard_map/all_gather | solution.py:62
  169.4 4.5 %reshape.31 = bf16[4,368640]{1,0:T(4,128)(2,1)} reshape(bf16[1280,1152]{1,0:T(8,128)(2,1)} %all-gather.6.cloned.1.call-done) | data formatting | bytes 5898240 | tf_op jit(solution)/shard_map/reshape | solution.py:64
  173.9 12.6 %fusion = bf16[16,368640]{1,0:T(8,128)(2,1)S(1)} fusion(bf16[4,368640]{1,0:T(4,128)(2,1)} %reshape.31, f32[4,32]{1,0:T(4,128)S(1)} %fusion.11, s32[]{:T(128)S(6)} %select_n.28), kind=kOutput, calls=%fused_computation.1 | convolution fusion | flops 294912000 | bytes 14746116 | tf_op jit(solution)/shard_map/dot_general | solution.py:65
  186.5 0.0 copy-start.1
  186.6 5.3 %copy.13 = bf16[2,8,320,1152]{3,2,1,0:T(8,128)(2,1)} copy(bf16[2,8,320,1152]{3,1,2,0:T(8,128)(2,1)S(1)} %bitcast.21) | data formatting | bytes 23592960
  191.8 0.0 copy-done.1
Async XLA Ops:
  7.2 2.1 %copy-start = (bf16[1,448,1280]{2,1,0:T(8,128)(2,1)S(1)}, bf16[1,448,1280]{2,1,0:T(8,128)(2,1)}, u32[]{:S(2)}) copy-start(bf16[1,448,1280]{2,1,0:T(8,128)(2,1)} %param.6) | copy-start | bytes 3440644
  7.2 72.5 %reduce-scatter.4.cloned.1.call-start = ((), (), s32[]{:S(2)}) async-start(), calls=%async_computation.4 | async-start | bytes 3686400 | tf_op jit(solution)/shard_map/reduce_scatter | solution.py:53
  19.4 122.4 %all-gather.4.cloned.1.call-start = ((), (), s32[]{:S(2)}) async-start(), calls=%async_computation.2 | async-start | bytes 3686400 | tf_op jit(solution)/shard_map/all_gather | solution.py:48
  19.5 13.7 %copy-start.3 = (f32[16,32]{1,0:T(8,128)S(1)}, f32[16,32]{1,0:T(8,128)}, u32[]{:S(2)}) copy-start(f32[16,32]{1,0:T(8,128)} %param.9) | copy-start | bytes 6148
  19.5 13.7 %copy-start.4 = (s32[4]{0:T(128)S(1)}, s32[4]{0:T(128)}, u32[]{:S(2)}) copy-start(s32[4]{0:T(128)} %param.10) | copy-start | bytes 52
  46.8 94.9 %copy-start.2 = (bf16[1,448,1152]{2,1,0:T(8,128)(2,1)S(1)}, bf16[1,448,1152]{2,1,0:T(8,128)(2,1)}, u32[]{:S(2)}) copy-start(bf16[1,448,1152]{2,1,0:T(8,128)(2,1)} %param.7) | copy-start | bytes 3096580
  70.5 98.9 %all-gather.6.cloned.1.call-start = ((), (), s32[]{:S(2)}) async-start(), calls=%async_computation.3 | async-start | bytes 3686400 | tf_op jit(solution)/shard_map/all_gather | solution.py:62
  186.5 5.3 %copy-start.1 = (bf16[1,448,1280]{2,1,0:T(8,128)(2,1)S(1)}, bf16[1,448,1280]{2,1,0:T(8,128)(2,1)}, u32[]{:S(2)}) copy-start(bf16[1,448,1280]{2,1,0:T(8,128)(2,1)} %param.6) | copy-start | bytes 3440644
Sparse Core Ops, SparseCore 0:
  19.5 60.0 reduce-scatter.3
  81.8 59.9 all-gather.3
  143.3 26.0 all-gather.5
where the time goes:
time: 199 us; the launch traced here: 198 us
  waiting for transfers between devices  94.3 us (47%)
  other arithmetic  30.4 us (15%)
  blocking collectives  22.3 us (11%)
  matrix products  22 us (11%)
  local copies, waits for them, and re-layouts  15.3 us (8%)
  between operations  13.8 us (7%)
    all_gather x1, waiting for transfers between devices, body(): lax.all_gather(merged_rows, 'edge', axis=0, tiled=True)  62.1 us
    all_gather x1, waiting for transfers between devices, body(): lax.all_gather(system_rows[None], ('expert', 'sys'), axis=0, tiled=True)  23.1 us
    all_to_all x1, blocking collectives, body(): lax.all_to_all(partials, 'expert', split_axis=0, concat_axis=0, tiled=True)  22.3 us
    convert_element_type x1, other arithmetic, body(): expert_weights.astype(jnp.float32)[None]  13.6 us
    reduce_sum x1, other arithmetic, body(): jnp.sum(own_coeffs[:, :, None, None] * expert_weights.astype(jnp.float32)...  13.5 us
    dot_general x1, matrix products, body(): folded = jnp.dot(local_coeffs, flat_rows, precision=highest)  12.6 us
    unnamed x12, local copies, waits for them, and re-layouts  10.7 us
    reduce_scatter x1, waiting for transfers between devices, body(): lax.psum_scatter(lax.dot_general(features, masked_grad, (((0,), (0,)), ((...  9.04 us
  transfers between devices with their start and end apart: 3, of which 3 were waited for; matrix products, arithmetic and copies ran while one was open for 17% of the time, Pallas kernels for 0%

commit v1 on v0

--- a/solution.py
+++ b/solution.py
@@ -59,7 +59,22 @@
         tiled=True,
     )
     local_coeffs = lax.dynamic_slice_in_dim(coeffs, expert_at * exp_local, exp_local, 1).T
-    block_rows = lax.all_gather(system_rows[None], ("expert", "sys"), axis=0, tiled=True)
+    size, place, rows = (
+        lax.axis_size(("expert", "sys")),
+        lax.axis_index(("expert", "sys")),
+        system_rows[None].shape[0],
+    )
+    forward = [(i, (i + 1) % size) for i in range(size)]
+    block_rows = jnp.zeros(
+        (*system_rows[None].shape[:0], size * rows, *system_rows[None].shape[0 + 1 :]),
+        system_rows[None].dtype,
+    )
+    current = system_rows[None]
+    for step in range(size):
+        owner = (place - step) % size
+        block_rows = lax.dynamic_update_slice_in_dim(block_rows, current, owner * rows, axis=0)
+        if step < size - 1:
+            current = lax.ppermute(current, ("expert", "sys"), forward)
     span_rows = block_rows.shape[0]
     flat_rows = block_rows.reshape(span_rows, -1).astype(jnp.float32)
     folded = jnp.dot(local_coeffs, flat_rows, precision=highest)

time: 199 us -> 184 us (0.925)
  waiting for transfers between devices: 94.3 us -> 79.2 us
    all_gather x1 -> x0, waiting for transfers between devices: 23.1 us -> none  [body(): lax.all_gather(system_rows[None], ('expert', 'sys'), axis=0, tiled=True)]
    ppermute x0 -> x3, waiting for transfers between devices: none -> 21.2 us  [body(): current = lax.ppermute(current, ('expert', 'sys'), forward)]
    all_gather x1, waiting for transfers between devices: 62.1 us -> 48.6 us  [body(): lax.all_gather(merged_rows, 'edge', axis=0, tiled=True)]
    unnamed x3, waiting for transfers between devices: 0.05 us -> 9.34 us
    reduce_scatter x1 -> x0, waiting for transfers between devices: 9.04 us -> none  [body(): lax.psum_scatter(lax.dot_general(features, masked_grad, (((0,), (0,)), ((...]
    reshape x1 -> x0, local copies, waits for them, and re-layouts: 4.52 us -> none  [body(): flat_rows = block_rows.reshape(span_rows, -1).astype(jnp.float32)]
    unnamed x12, local copies, waits for them, and re-layouts: 10.7 us -> 14.7 us
  transfers between devices with their start and end apart: 3 -> 5, of which waited for: 3 -> 4; matrix products, arithmetic and copies ran while one was open for 17% -> 20% of each run, Pallas kernels for 0% -> 0%
where the time goes in v1:
time: 184 us; the launch traced here: 183 us
  waiting for transfers between devices  79.2 us (43%)
  other arithmetic  30.4 us (17%)
  blocking collectives  22.2 us (12%)
  matrix products  20.9 us (11%)
  local copies, waits for them, and re-layouts  16.2 us (9%)
  between operations  14.2 us (8%)
    all_gather x1, waiting for transfers between devices, body(): lax.all_gather(merged_rows, 'edge', axis=0, tiled=True)  48.6 us
    all_to_all x1, blocking collectives, body(): lax.all_to_all(partials, 'expert', split_axis=0, concat_axis=0, tiled=True)  22.2 us
    ppermute x3, waiting for transfers between devices, body(): current = lax.ppermute(current, ('expert', 'sys'), forward)  21.2 us
    unnamed x12, local copies, waits for them, and re-layouts  14.7 us
    convert_element_type x1, other arithmetic, body(): expert_weights.astype(jnp.float32)[None]  13.6 us
    reduce_sum x1, other arithmetic, body(): jnp.sum(own_coeffs[:, :, None, None] * expert_weights.astype(jnp.float32)...  13.5 us
    dot_general x1, matrix products, body(): folded = jnp.dot(local_coeffs, flat_rows, precision=highest)  11.2 us
    unnamed x3, waiting for transfers between devices  9.34 us
  transfers between devices with their start and end apart: 5, of which 4 were waited for; matrix products, arithmetic and copies ran while one was open for 20% of the time, Pallas kernels for 0%

profile of v1, /device:TPU:0, one launch (start us, length us, event | category | flops | bytes accessed | tf_op | source)
XLA Modules:
  0.0 183.2 jit_solution(4136641017780971516)
XLA Ops:
  7.2 0.0 copy-start
  7.2 0.0 reduce-scatter.4.cloned.1.call-start
  7.2 1.4 fusion.14
  8.6 0.7 add_compare_fusion
  9.3 0.0 copy-done
  9.3 4.6 %fusion.1 = bf16[1280,1152]{0,1:T(8,128)(2,1)} fusion(bf16[1,448,1280]{2,1,0:T(8,128)(2,1)S(1)} %copy-done, bf16[1,448,1152]{2,1,0:T(8,128)(2,1)} %param.7, pred[448]{0:T(512)(128)(4,1)S(1)} %add_compare_fusion), kind=kOutput, calls=%fused_computation.4 | convolution fusion | flops 1323196416 | bytes 5128640 | tf_op jit(solution)/shard_map/dot_general | solution.py:54
  13.9 5.4 %copy.16 = bf16[1280,1152]{1,0:T(8,128)(2,1)} copy(bf16[1280,1152]{0,1:T(8,128)(2,1)} %fusion.1) | data formatting | bytes 5898240
  19.4 0.0 reduce-scatter.4.cloned.1.call-update
  19.4 0.0 all-gather.2.cloned.1.call-start
  19.4 0.0 copy-start.2
  19.5 0.0 copy-start.3
  19.5 13.6 %convert_element_type.25 = f32[16,320,1152]{2,1,0:T(8,128)} convert(bf16[16,320,1152]{2,1,0:T(8,128)(2,1)} %param.8) | non-fusion elementwise | flops 5898240 | bytes 35389440 | tf_op jit(solution)/shard_map/convert_element_type | solution.py:38
  33.1 0.0 copy-done.2
  33.1 0.0 copy-done.3
  33.1 0.2 fusion.11
  33.3 0.1 constant_dynamic-slice_fusion
  33.3 13.5 %multiply_reduce_fusion = bf16[2,320,1152]{2,1,0:T(8,128)(2,1)S(1)} fusion(f32[16,320,1152]{2,1,0:T(8,128)} %convert_element_type.25, f32[2,16]{1,0:T(2,128)S(1)} %bitcast.30), kind=kLoop, calls=%fused_computation.2 | loop fusion | flops 22855680 | bytes 25067648 | tf_op jit(solution)/shard_map/reduce_sum | solution.py:37
  46.8 22.2 %all_to_all.5 = bf16[2,320,1152]{2,1,0:T(8,128)(2,1)S(1)} all-to-all(bf16[2,320,1152]{2,1,0:T(8,128)(2,1)S(1)} %multiply_reduce_fusion), channel_id=1, replica_groups=mesh['groups'=2,'edge'=4,'expert'=2,'sys'=2] {'expert'}, dimensions={0} | all-to-all | bytes 2949120 | tf_op jit(solution)/shard_map/all_to_all | solution.py:41
  69.0 1.3 reduce_sum.32
  70.3 0.0 all-gather.2.cloned.1.call-update
  70.3 9.3 %reduce-scatter.4.cloned.1.call-done = bf16[320,1152]{1,0:T(8,128)(2,1)} async-done(((bf16[1280,1152]{1,0:T(8,128)(2,1)}), bf16[320,1152]{1,0:T(8,128)(2,1)}) %reduce-scatter.4.cloned.1.call-update) | async-done | bytes 737296
  79.6 1.7 copy.17
  81.4 0.8 copy.14
  82.2 0.1 collective-permute-start
  82.3 10.9 %collective-permute-done = bf16[1,320,1152]{2,1,0:T(8,128)(2,1)S(1)} collective-permute-done((bf16[1,320,1152]{2,1,0:T(8,128)(2,1)S(1)}, bf16[1,320,1152]{2,1,0:T(8,128)(2,1)S(1)}, u32[]{:S(2)}, u32[]{:S(2)}) %collective-permute-start) | collective-permute-done | bytes 737312 | tf_op jit(solution)/shard_map/ppermute | solution.py:77
  93.1 0.0 collective-permute-start.1
  93.1 48.6 %all-gather.2.cloned.1.call-done = bf16[1280,1152]{1,0:T(8,128)(2,1)} async-done(((bf16[320,1152]{1,0:T(8,128)(2,1)}), bf16[1280,1152]{1,0:T(8,128)(2,1)}) %all-gather.2.cloned.1.call-update) | async-done | bytes 2949136 | tf_op jit(solution)/shard_map/all_gather | solution.py:48
  141.8 4.9 %fusion.2 = bf16[1,448,1280]{2,1,0:T(8,128)(2,1)} fusion(bf16[1280,1152]{1,0:T(8,128)(2,1)} %all-gather.2.cloned.1.call-done, bf16[1,448,1152]{2,1,0:T(8,128)(2,1)} %param.7, pred[448]{0:T(512)(128)(4,1)S(1)} %add_compare_fusion), kind=kOutput, calls=%fused_computation.6 | convolution fusion | flops 1322295296 | bytes 5128640 | tf_op jit(solution)/shard_map/dot_general | solution.py:46
  146.6 0.0 collective-permute-done.1
  146.6 0.0 collective-permute-start.2
  146.6 0.2 broadcast_in_dim.38
  146.9 0.1 constant_dynamic-update-slice_fusion.3
  147.0 0.1 constant_dynamic-update-slice_fusion.2
  147.1 0.1 constant_dynamic-update-slice_fusion.1
  147.2 10.3 %collective-permute-done.2 = bf16[1,320,1152]{2,1,0:T(8,128)(2,1)S(1)} collective-permute-done((bf16[1,320,1152]{2,1,0:T(8,128)(2,1)S(1)}, bf16[1,320,1152]{2,1,0:T(8,128)(2,1)S(1)}, u32[]{:S(2)}, u32[]{:S(2)}) %collective-permute-start.2) | collective-permute-done | bytes 737312 | tf_op jit(solution)/shard_map/ppermute | solution.py:77
  157.5 0.1 constant_dynamic-update-slice_fusion
  157.6 2.3 %copy.18 = bf16[1,4,320,1152]{3,1,2,0:T(4,128)(2,1)S(1)} copy(bf16[1,4,320,1152]{3,2,1,0:T(8,128)(2,1)S(1)} %bitcast.27) | data formatting | bytes 5898240
  159.9 11.2 %fusion = bf16[16,368640]{1,0:T(8,128)(2,1)S(1)} fusion(bf16[4,368640]{1,0:T(4,128)(2,1)S(1)} %bitcast.25, f32[4,32]{1,0:T(4,128)S(1)} %fusion.11, s32[]{:T(128)S(6)} %select_n.59), kind=kOutput, calls=%fused_computation.1 | convolution fusion | flops 294912000 | bytes 14746116 | tf_op jit(solution)/shard_map/dot_general | solution.py:80
  171.1 0.0 copy-start.1
  171.1 5.3 %copy.19 = bf16[2,8,320,1152]{3,2,1,0:T(8,128)(2,1)} copy(bf16[2,8,320,1152]{3,1,2,0:T(8,128)(2,1)S(1)} %bitcast.24) | data formatting | bytes 23592960
  176.3 0.0 copy-done.1
Async XLA Ops:
  7.2 2.1 %copy-start = (bf16[1,448,1280]{2,1,0:T(8,128)(2,1)S(1)}, bf16[1,448,1280]{2,1,0:T(8,128)(2,1)}, u32[]{:S(2)}) copy-start(bf16[1,448,1280]{2,1,0:T(8,128)(2,1)} %param.6) | copy-start | bytes 3440644
  7.2 72.5 %reduce-scatter.4.cloned.1.call-start = ((), (), s32[]{:S(2)}) async-start(), calls=%async_computation.3 | async-start | bytes 3686400
  19.4 122.4 %all-gather.2.cloned.1.call-start = ((), (), s32[]{:S(2)}) async-start(), calls=%async_computation.2 | async-start | bytes 3686400 | tf_op jit(solution)/shard_map/all_gather | solution.py:48
  19.4 13.6 %copy-start.2 = (f32[16,32]{1,0:T(8,128)S(1)}, f32[16,32]{1,0:T(8,128)}, u32[]{:S(2)}) copy-start(f32[16,32]{1,0:T(8,128)} %param.9) | copy-start | bytes 6148
  19.5 13.6 %copy-start.3 = (s32[4]{0:T(128)S(1)}, s32[4]{0:T(128)}, u32[]{:S(2)}) copy-start(s32[4]{0:T(128)} %param.10) | copy-start | bytes 52
  82.2 10.9 %collective-permute-start = (bf16[1,320,1152]{2,1,0:T(8,128)(2,1)S(1)}, bf16[1,320,1152]{2,1,0:T(8,128)(2,1)S(1)}, u32[]{:S(2)}, u32[]{:S(2)}) collective-permute-start(bf16[1,320,1152]{2,1,0:T(8,128)(2,1)S(1)} %copy.14), channel_id=1, source_target_pairs={{0,1},{1,2},{2,3},{3,0},{4,5},{5,6},{6,7},{7,4},{8,9},{9,10},{10,1... | collective-permute-start | bytes 2211848 | tf_op jit(solution)/shard_map/ppermute | solution.py:77
  93.1 53.5 %collective-permute-start.1 = (bf16[1,320,1152]{2,1,0:T(8,128)(2,1)S(1)}, bf16[1,320,1152]{2,1,0:T(8,128)(2,1)S(1)}, u32[]{:S(2)}, u32[]{:S(2)}) collective-permute-start(bf16[1,320,1152]{2,1,0:T(8,128)(2,1)S(1)} %collective-permute-done), channel_id=1, source_target_pairs={{0,1},{1,2},{2,3},{3,0},{4,5},{5,6},{6,7},{7,4},{8,9},{9,10},{10,1... | collective-permute-start | bytes 2211848 | tf_op jit(solution)/shard_map/ppermute | solution.py:77
  146.6 10.9 %collective-permute-start.2 = (bf16[1,320,1152]{2,1,0:T(8,128)(2,1)S(1)}, bf16[1,320,1152]{2,1,0:T(8,128)(2,1)S(1)}, u32[]{:S(2)}, u32[]{:S(2)}) collective-permute-start(bf16[1,320,1152]{2,1,0:T(8,128)(2,1)S(1)} %collective-permute-done.1), channel_id=1, source_target_pairs={{0,1},{1,2},{2,3},{3,0},{4,5},{5,6},{6,7},{7,4},{8,9},{9,10},{10,1... | collective-permute-start | bytes 2211848 | tf_op jit(solution)/shard_map/ppermute | solution.py:77
  171.1 5.3 %copy-start.1 = (bf16[1,448,1280]{2,1,0:T(8,128)(2,1)S(1)}, bf16[1,448,1280]{2,1,0:T(8,128)(2,1)}, u32[]{:S(2)}) copy-start(bf16[1,448,1280]{2,1,0:T(8,128)(2,1)} %param.6) | copy-start | bytes 3440644
Sparse Core Ops, SparseCore 0:
  19.5 60.0 reduce-scatter.3
  81.8 59.9 all-gather.1
